TPU v7x, 512 devices: a whole 4x4x16 slice. The times are simulated.
512 devices in a mesh: src: 16 (over y_hi, x, core), rcv: 32 (over y_lo, z).
Axes of the slice: x: 4, y: 4 (y_hi: 2, y_lo: 2; y = y_hi * 2 + y_lo), z: 16, core: 2. Of those that a mesh axis runs over, the one named last changes fastest.
Arguments:
- spectra: bfloat16 [2, 8, 192, 8192], P(None, None, 'src', 'rcv'), as said below
- alive: int32 [192, 8192], P('src', 'rcv'), may hold values 0 or 1
Outputs:
- stacked: bfloat16 [2, 8, 8192, 8192], P(None, None, 'src', 'rcv')
Inputs may be any that keep to these rules, and one draw needn't show every extreme that they name: spectra: every entry is a random factor times an amplitude of its window and channel that spreads over a factor of 15.
All inputs are finite; a program needn't handle non-finite values. No bound on the sum of `alive` on one device may be relied on, other than what follows from the above.
Results may differ from a plain program's by a relative error of at most 0.0057.
Values may be sent and summed in bfloat16 or wider, within the bound.
No kernel may reach another device: no remote copies, remote signals or barrier semaphores. Data moves between devices by JAX's collectives and lax.ppermute only.
A program may use at most 64 MiB of HBM per device.

v0:
```python
import jax
import jax.numpy as jnp
from jax import lax
from jax.sharding import PartitionSpec as P


def spread(block, axis, holder):
    block = jnp.where(lax.axis_index(axis) == holder, block, jnp.zeros_like(block))
    return lax.psum(block, axis)


def whiten(spectra, alive, bins):
    values = spectra.astype(jnp.float32)
    power = jnp.sum(values * values, axis=(0, 1)) / bins
    factor = alive.astype(jnp.float32) / jnp.sqrt(jnp.maximum(power, 0.5))
    return (values * factor).astype(jnp.bfloat16)


def cross_terms(source_part, receiver_part):
    swapped = jnp.stack((receiver_part[1], -receiver_part[0]))
    real_sum = jnp.einsum(
        "kfwc,kfwd->fcd", source_part, receiver_part, preferred_element_type=jnp.float32
    )
    imag_sum = jnp.einsum(
        "kfwc,kfwd->fcd", source_part, swapped, preferred_element_type=jnp.float32
    )
    return jnp.stack((real_sum, imag_sum))


def body(spectra, alive):
    bins = spectra.shape[1]
    whitened = whiten(spectra, alive, bins)
    ratio = lax.axis_size("rcv") // lax.axis_size("src")
    row_index = lax.axis_index("src")
    receivers = lax.all_gather(whitened, "src", axis=2, tiled=True)
    blocks = []
    for offset in range(ratio):
        blocks.append(spread(receivers, "rcv", row_index * ratio + offset))
    sources = jnp.concatenate(blocks, axis=3)
    stacked = cross_terms(sources, receivers)
    total_windows = receivers.shape[2]
    factor = jnp.float32(1.0) / jnp.sqrt(jnp.float32(total_windows))
    return (stacked * factor).astype(jnp.bfloat16)


def solution(mesh):
    return jax.shard_map(
        body,
        mesh=mesh,
        in_specs=(P(None, None, "src", "rcv"), P("src", "rcv")),
        out_specs=P(None, None, "src", "rcv"),
        check_vma=False,
    )
```

profile of v0, /device:TPU:2, one launch (start us, length us, event | category | flops | bytes accessed | tf_op | source)
XLA Modules:
  0.0 363.6 jit_solution(11212525343441608051)
XLA Ops:
  6.5 0.0 all-gather.2.cloned.1.call-start
  6.5 0.9 fusion.4
  7.5 0.7 rsqrt_multiply_fusion
  8.2 1.6 fusion.5
  9.8 0.0 all-gather.2.cloned.1.call-update
  9.8 0.0 all-reduce.3.cloned.1.call-start
  9.8 67.1 %all-gather.2.cloned.1.call-done = bf16[2,8,192,256]{3,1,0,2:T(8,128)(2,1)} async-done(((bf16[2,8,12,256]{3,1,0,2:T(8,128)(2,1)}), bf16[2,8,192,256]{3,1,0,2:T(8,128)(2,1)}) %all-gather.2.cloned.1.call-update) | async-done | bytes 1572880 | tf_op jit(solution)/shard_map/all_gather | solution.py:35
  77.0 4.1 %fusion.9 = (bf16[2,8,192,256]{3,2,0,1:T(8,128)(2,1)S(1)}, bf16[2,8,192,256]{3,2,0,1:T(8,128)(2,1)}, bf16[2,8,192,256]{3,2,0,1:T(8,128)(2,1)}) fusion(bf16[2,8,192,256]{3,1,0,2:T(8,128)(2,1)} %all-gather.2.cloned.1.call-done, pred[]{:T(512)S(6)} %eq.6, pred[]{:T(512)S(6)} %eq.7), kind=kLoop, calls=%fused_computation.20 | loop fusion | flops 1572864 | bytes 6291458 | tf_op jit(solution)/shard_map/all_gather | solution.py:35
  81.1 0.0 all-reduce.3.cloned.1.call-update
  81.1 0.1 fusion.8
  81.2 267.8 %all-reduce.3.cloned.1.call-done = (bf16[2,8,192,256]{3,2,0,1:T(8,128)(2,1)}, bf16[2,8,192,256]{3,2,0,1:T(8,128)(2,1)}) async-done(((bf16[2,8,192,256]{3,2,0,1:T(8,128)(2,1)}, bf16[2,8,192,256]{3,2,0,1:T(8,128)(2,1)}), (bf16[2,8,192,256]{3,2,0,1:T(8,128)(2,1)}, bf16[2,8,192,256]{3,2,0,1:T(8,128)(2,1)})) %all-reduce.3.cloned.1.call-update) | async-done | bytes 3145744 | tf_op jit(solution)/shard_map/psum | solution.py:9
  349.0 0.0 copy-start.1
  349.0 1.7 constant_dynamic-update-slice_fusion.1
  350.7 0.2 copy-done.1
  350.9 0.1 constant_dynamic-update-slice_fusion
  351.1 0.0 copy-start
  351.1 1.4 convolution_bitcast_fusion
  352.5 0.0 copy-done
  352.5 1.6 convolution_bitcast_fusion.1
  354.2 2.6 fusion
Async XLA Ops:
  6.5 70.4 %all-gather.2.cloned.1.call-start = ((), (), s32[]{:S(2)}) async-start(), calls=%async_computation | async-start | bytes 1671168 | tf_op jit(solution)/shard_map/all_gather | solution.py:35
  9.8 339.3 %all-reduce.3.cloned.1.call-start = ((), (), s32[]{:S(2)}) async-start(), calls=%async_computation.1 | async-start | bytes 6291456 | tf_op jit(solution)/shard_map/psum | solution.py:9
  349.0 1.9 copy-start.1
  351.1 1.5 copy-start
Sparse Core Ops, SparseCore 0:
  10.7 66.2 all-gather.1
  81.2 267.7 all-reduce.2
where the time goes:
time: 364 us
  waiting for transfers between devices  335 us (92%)
  between operations  13.5 us (4%)
  other arithmetic  9.98 us (3%)
    psum x1, waiting for transfers between devices, spread(): return lax.psum(block, axis)  268 us
    all_gather x1, waiting for transfers between devices, body(): receivers = lax.all_gather(whitened, 'src', axis=2, tiled=True)  67.1 us
  transfers between devices with their start and end apart: 2, of which 2 were waited for; matrix products, arithmetic and copies ran while one was open for 0% of the time, Pallas kernels for 0%

commit v1 on v0

--- a/solution.py
+++ b/solution.py
@@ -32,7 +32,9 @@
     whitened = whiten(spectra, alive, bins)
     ratio = lax.axis_size("rcv") // lax.axis_size("src")
     row_index = lax.axis_index("src")
-    receivers = lax.all_gather(whitened, "src", axis=2, tiled=True)
+    receivers = jnp.concatenate(
+        lax.all_to_all(jnp.stack([whitened] * lax.axis_size("src")), "src", 0, 0), axis=2
+    )
     blocks = []
     for offset in range(ratio):
         blocks.append(spread(receivers, "rcv", row_index * ratio + offset))

time: 364 us -> 327 us (0.90)
  waiting for transfers between devices: 335 us -> 290 us
  starting transfers between devices: 0.04 us -> 9.45 us
    all_gather x1 -> x0, waiting for transfers between devices: 67.1 us -> none  [body(): receivers = lax.all_gather(whitened, 'src', axis=2, tiled=True)]
    all_to_all x0 -> x1, waiting for transfers between devices: none -> 20.8 us  [body(): lax.all_to_all(jnp.stack([whitened] * lax.axis_size('src')), 'src', 0, 0)]
    all_to_all x0 -> x1, starting transfers between devices: none -> 9.41 us  [body(): lax.all_to_all(jnp.stack([whitened] * lax.axis_size('src')), 'src', 0, 0)]
    all_gather x1 -> x0, other arithmetic: 4.1 us -> none  [body(): receivers = lax.all_gather(whitened, 'src', axis=2, tiled=True)]
where the time goes in v1:
time: 327 us
  waiting for transfers between devices  290 us (89%)
  between operations  13.5 us (4%)
  starting transfers between devices  9.45 us (3%)
  other arithmetic  7.52 us (2%)
  local copies, waits for them, and re-layouts  3.74 us (1%)
    psum x1, waiting for transfers between devices, spread(): return lax.psum(block, axis)  269 us
    all_to_all x1, waiting for transfers between devices, body(): lax.all_to_all(jnp.stack([whitened] * lax.axis_size('src')), 'src', 0, 0)  20.8 us
    all_to_all x1, starting transfers between devices, body(): lax.all_to_all(jnp.stack([whitened] * lax.axis_size('src')), 'src', 0, 0)  9.41 us
  transfers between devices with their start and end apart: 2, of which 2 were waited for; matrix products, arithmetic and copies ran while one was open for 0% of the time, Pallas kernels for 0%

profile of v1, /device:TPU:2, one launch (start us, length us, event | category | flops | bytes accessed | tf_op | source)
XLA Modules:
  0.0 327.2 jit_solution(8340391568233328419)
XLA Ops:
  6.5 0.9 fusion.5
  7.5 0.7 rsqrt_multiply_fusion
  8.2 0.9 fusion.6
  9.1 1.3 stack.10
  10.4 9.4 %all-to-all-start = ((bf16[16,2,8,12,256]{4,2,3,1,0:T(8,128)(2,1)}), bf16[16,2,8,12,256]{4,2,3,1,0:T(8,128)(2,1)S(1)}, u32[]{:S(2)}, u32[]{:S(2)}) async-start(bf16[16,2,8,12,256]{4,2,3,1,0:T(8,128)(2,1)} %stack.10), calls=%async_computation | async-start | bytes 3145728 | tf_op jit(solution)/shard_map/all_to_all | solution.py:36
  19.9 0.0 all-reduce.3.cloned.1.call-start
  19.9 20.8 %all-to-all-done = bf16[16,2,8,12,256]{4,2,3,1,0:T(8,128)(2,1)S(1)} async-done(((bf16[16,2,8,12,256]{4,2,3,1,0:T(8,128)(2,1)}), bf16[16,2,8,12,256]{4,2,3,1,0:T(8,128)(2,1)S(1)}, u32[]{:S(2)}, u32[]{:S(2)}) %all-to-all-start) | async-done | bytes 1572896 | tf_op jit(solution)/shard_map/all_to_all | solution.py:36
  40.7 0.1 copy.23
  40.8 2.3 broadcast_select_fusion
  43.1 0.0 all-reduce.3.cloned.1.call-update
  43.1 0.1 fusion.8
  43.2 0.2 copy.13
  43.4 0.2 copy.14
  43.6 269.2 %all-reduce.3.cloned.1.call-done = (bf16[2,8,192,256]{3,2,0,1:T(8,128)(2,1)}, bf16[2,8,192,256]{3,2,0,1:T(8,128)(2,1)}) async-done(((bf16[2,8,192,256]{3,2,0,1:T(8,128)(2,1)}, bf16[2,8,192,256]{3,2,0,1:T(8,128)(2,1)}), (bf16[2,8,192,256]{3,2,0,1:T(8,128)(2,1)}, bf16[2,8,192,256]{3,2,0,1:T(8,128)(2,1)})) %all-reduce.3.cloned.1.call-update) | async-done | bytes 3145744 | tf_op jit(solution)/shard_map/psum | solution.py:9
  312.8 0.0 copy-start
  312.8 1.7 constant_dynamic-update-slice_fusion.1
  314.5 0.2 copy-done
  314.7 0.1 constant_dynamic-update-slice_fusion
  314.8 1.5 convolution_bitcast_fusion.1
  316.3 1.4 convolution_bitcast_fusion
  317.8 2.6 fusion
Async XLA Ops:
  10.4 30.3 %all-to-all-start = ((bf16[16,2,8,12,256]{4,2,3,1,0:T(8,128)(2,1)}), bf16[16,2,8,12,256]{4,2,3,1,0:T(8,128)(2,1)S(1)}, u32[]{:S(2)}, u32[]{:S(2)}) async-start(bf16[16,2,8,12,256]{4,2,3,1,0:T(8,128)(2,1)} %stack.10), calls=%async_computation | async-start | bytes 3145728 | tf_op jit(solution)/shard_map/all_to_all | solution.py:36
  19.9 292.9 %all-reduce.3.cloned.1.call-start = ((), (), s32[]{:S(2)}) async-start(), calls=%async_computation.1 | async-start | bytes 6291456 | tf_op jit(solution)/shard_map/psum | solution.py:9
  312.8 1.9 copy-start
Sparse Core Ops, SparseCore 0:
  43.2 269.4 all-reduce.2
